TPU v7x, 32 devices: a whole 2x2x4 slice. The times are simulated.
32 devices in a mesh: leaf: 8 (over z, x), vec: 4 (over y, core).
Axes of the slice: x: 2, y: 2, z: 4, core: 2. Of those that a mesh axis runs over, the one named last changes fastest.
Arguments:
- vectors: float32 [32, 65536], P('vec', 'leaf'), may hold values from -15 to 15
- coords: float32 [3, 65536], P(None, 'leaf'), may hold values from 0 to 64, as said below
- leaf_basis: float32 [32, 65536], P(None, 'leaf'), may hold values from -0.375 to 0.375
- node_ops: float32 [496, 32, 128], P('leaf'), may hold values from -0.75 to 0.75
- top_ops: float32 [2, 32, 192], replicated, may hold values from -0.75 to 0.75
- near_target: int32 [1280], P('leaf'), may hold values from 0 to 255, as said below
- near_source: int32 [1280], P('leaf'), may hold values from 0 to 255, as said below
- near_count: int32 [8], P('leaf'), may hold values from 64 to 160, as said below
Outputs:
- product: float32 [32, 65536], P('vec', 'leaf')
- gram_matrix: float32 [32, 32], P(None, 'vec')
Inputs may be any that keep to these rules, and one draw needn't show every extreme that they name: `near_target`: slots of one index of leaf name target leaves of that index only; each aligned block of 32 slots of an index names each of its leaves once; in the first run every leaf is paired with itself, and in the second run the first leaf of each index is paired with the leaf just below it and the last leaf with the leaf just above it, where those exist. `near_source`: A source leaf lies within 4 leaves of its target leaf; no pair repeats within one index of leaf. The first near_count[d] slots of index d are live, the rest are padding; some index fills all 160 slots. `coords`: point k lies in the box of its leaf l = k // 256: first coordinate from 0.25 l to 0.25 (l + 1), the other two from 0 to 1.
All inputs are finite; a program needn't handle non-finite values.
Results may differ from a plain program's by a relative error of at most 0.0003.
Values sent between devices are 32-bit elements; how exact they have to be, the bound alone decides.
A program may use at most 64 MiB of HBM per device.

v0:
```python
import jax
import jax.numpy as jnp
import numpy as np
from jax import lax
from jax.sharding import PartitionSpec as P

PTS = 256
NEAR_REACH = 4


EXACT_ARITHMETIC = lax.Precision.HIGHEST
SIGNAL = 0.1
NUGGET = 0.5
LENGTH = 0.35
EVEN_OFFSETS = (-2, 2, 3)
ODD_OFFSETS = (-3, -2, 2)


def padded_2(block, sides, width):
    for axis, dim in sides:
        count = lax.axis_size(axis)
        forward = [(i, i + 1) for i in range(count - 1)]
        backward = [(target, source) for source, target in forward]
        low = lax.ppermute(
            lax.slice_in_dim(block, block.shape[dim] - width, None, axis=dim), axis, forward
        )
        high = lax.ppermute(lax.slice_in_dim(block, 0, width, axis=dim), axis, backward)
        block = jnp.concatenate([low, block, high], axis=dim)
    return block


def matern(target_pts, source_pts):
    pair_separation = jnp.zeros(
        (target_pts.shape[1], target_pts.shape[2], source_pts.shape[2]), jnp.float32
    )
    for axis_id in range(3):
        spacing = target_pts[axis_id][:, :, None] - source_pts[axis_id][:, None, :]
        pair_separation = pair_separation + spacing * spacing
    scaled = jnp.sqrt(3.0 * pair_separation) / LENGTH
    return SIGNAL * (1.0 + scaled) * jnp.exp(-scaled)


def take_rows(padded, count_nodes, pad_width):
    parity_ids = np.arange(count_nodes) % 2
    gathered = []
    for slot_index in range(3):
        shift_by = np.where(parity_ids == 0, EVEN_OFFSETS[slot_index], ODD_OFFSETS[slot_index])
        gathered.append(padded[np.arange(count_nodes) + shift_by + pad_width])
    return jnp.stack(gathered, axis=1)


def couple_level(padded, operators, count_nodes, pad_width, rank_size):
    sources = take_rows(padded, count_nodes, pad_width)
    blocks = operators[:, :, : 3 * rank_size].reshape(count_nodes, rank_size, 3, rank_size)
    return jnp.einsum("navr,nras->nvs", sources, blocks, precision=EXACT_ARITHMETIC)


def raise_level(incoming_coefficients, operators, rank_size):
    moved = jnp.einsum(
        "nvr,nrs->nvs",
        incoming_coefficients,
        operators[:, :, 3 * rank_size :],
        precision=EXACT_ARITHMETIC,
    )
    return moved[0::2] + moved[1::2]


def lower_level(field_in, operators, rank_size):
    spread = jnp.repeat(field_in, 2, axis=0)
    return jnp.einsum(
        "nvs,nrs->nvr", spread, operators[:, :, 3 * rank_size :], precision=EXACT_ARITHMETIC
    )


def through(incoming_coefficients, operators, position, rank_size):
    return jnp.einsum(
        "...r,rs->...s",
        incoming_coefficients,
        operators[:, position * rank_size : (position + 1) * rank_size],
        precision=EXACT_ARITHMETIC,
    )


def couple_top(partners, operators, parity, rank_size):
    far_left, near_left, near_right, far_right = partners
    outer = jnp.where(
        parity == 0,
        through(far_right, operators, 3, rank_size),
        through(far_left, operators, 0, rank_size),
    )
    return (
        through(near_left, operators, 1, rank_size)
        + through(near_right, operators, 2, rank_size)
        + outer
    )


def raise_pair(left_coef, right_coef, operators, rank_size):
    return through(left_coef, operators, 4, rank_size) + through(
        right_coef, operators, 5, rank_size
    )


def lower_top(field_in, operators, parity, rank_size):
    even_part = jnp.einsum(
        "...s,rs->...r",
        field_in,
        operators[:, 4 * rank_size : 5 * rank_size],
        precision=EXACT_ARITHMETIC,
    )
    odd_part = jnp.einsum(
        "...s,rs->...r",
        field_in,
        operators[:, 5 * rank_size : 6 * rank_size],
        precision=EXACT_ARITHMETIC,
    )
    return jnp.where(parity == 0, even_part, odd_part)


def near_field(window, local_coords, targets, sources, weights, pair_block):
    columns = window.shape[0] - 3
    leaves_dev = local_coords.shape[1]
    step_count = targets.shape[0] // pair_block

    def add_block(accumulated_sum, portion):
        target_ids, source_ids, live_mask = portion
        source_rows = jnp.take(window, source_ids, axis=1)
        target_pts = jnp.take(local_coords, target_ids, axis=1)
        kernel = matern(target_pts, source_rows[columns:])
        contribution = jnp.einsum(
            "vbs,bts->bvt", source_rows[:columns], kernel, precision=EXACT_ARITHMETIC
        )
        selection_mask = (target_ids[:, None] == jnp.arange(leaves_dev)[None, :]).astype(
            jnp.float32
        ) * live_mask[:, None]
        return (
            accumulated_sum
            + jnp.einsum("qs,qhg->hsg", selection_mask, contribution, precision=EXACT_ARITHMETIC),
            None,
        )

    initial = jnp.zeros((columns, leaves_dev, window.shape[2]), jnp.float32)
    portions = (
        targets.reshape(step_count, pair_block),
        sources.reshape(step_count, pair_block),
        weights.reshape(step_count, pair_block),
    )
    accumulated_sum, unused = lax.scan(add_block, initial, portions)
    return accumulated_sum.reshape(columns, leaves_dev * window.shape[2])


def on_device(vectors, coords, leaf_basis, node_ops, top_ops, near_target, near_source, near_count):
    rank_size = leaf_basis.shape[0]
    columns_dev = vectors.shape[0]
    points_dev = vectors.shape[1]
    leaves_dev = points_dev // PTS
    device = lax.axis_index("leaf")
    vec_index = lax.axis_index("vec")
    vec_count = lax.axis_size("vec")
    leaf_count = lax.axis_size("leaf")
    all_columns = lax.all_gather(vectors, "vec", axis=0, tiled=True)
    base_leaf = device * leaves_dev
    slot_ids = jnp.arange(near_target.shape[0], dtype=jnp.int32)
    live_all = (slot_ids < near_count[0]).astype(jnp.float32)
    target_all = near_target - base_leaf
    source_all = near_source - base_leaf + NEAR_REACH
    local_coords = coords.reshape(3, leaves_dev, PTS)
    stacked = jnp.concatenate([all_columns, coords], axis=0)
    window = padded_2(stacked, (("leaf", 1),), NEAR_REACH * PTS)
    window = window.reshape(all_columns.shape[0] + 3, leaves_dev + 2 * NEAR_REACH, PTS)
    share_count = near_target.shape[0] // vec_count
    slot_grid = slot_ids.reshape(share_count, vec_count)
    picked = lax.dynamic_slice_in_dim(slot_grid, vec_index, 1, 1)[:, 0]
    partial_sum = near_field(
        window,
        local_coords,
        target_all[picked],
        source_all[picked],
        live_all[picked],
        share_count // (leaves_dev // vec_count),
    )
    near_part = lax.psum_scatter(partial_sum, "vec", scatter_dimension=0, tiled=True)
    leaf_basis_matrix = leaf_basis.reshape(rank_size, leaves_dev, PTS)
    current = jnp.einsum(
        "vlp,rlp->lvr",
        vectors.reshape(columns_dev, leaves_dev, PTS),
        leaf_basis_matrix,
        precision=EXACT_ARITHMETIC,
    )
    level_ops = []
    level_fields = []
    offset_node = 0
    nodes_here = leaves_dev
    while nodes_here >= 2:
        ops_here = node_ops[offset_node : offset_node + nodes_here]
        rim_width = min(3, nodes_here)
        padded = padded_2(current, (("leaf", 0),), rim_width)
        level_fields.append(couple_level(padded, ops_here, nodes_here, rim_width, rank_size))
        level_ops.append(ops_here)
        current = raise_level(current, ops_here, rank_size)
        offset_node += nodes_here
        nodes_here //= 2
    top_levels = top_ops.shape[0]
    top_fields = []
    all_roots = lax.all_gather(current, "leaf", axis=0, tiled=True)
    for height in range(top_levels):
        padded_top = jnp.pad(all_roots, ((3, 3), (0, 0), (0, 0)))
        node_id = device // (1 << height)
        near_rows = lax.dynamic_slice_in_dim(padded_top, node_id, 7, 0)
        partners = (near_rows[0], near_rows[1], near_rows[5], near_rows[6])
        top_fields.append(couple_top(partners, top_ops[height], node_id % 2, rank_size))
        if height + 1 < top_levels:
            all_roots = raise_pair(all_roots[0::2], all_roots[1::2], top_ops[height], rank_size)
    downward = top_fields[top_levels - 1]
    for height in range(top_levels - 2, -1, -1):
        parity = device // (1 << height) % 2
        downward = top_fields[height] + lower_top(downward, top_ops[height], parity, rank_size)
    downward = downward[None]
    for index_level in range(len(level_fields) - 1, -1, -1):
        downward = level_fields[index_level] + lower_level(
            downward, level_ops[index_level], rank_size
        )
    far_part = jnp.einsum(
        "lvr,rlp->vlp", downward, leaf_basis_matrix, precision=EXACT_ARITHMETIC
    ).reshape(columns_dev, points_dev)
    product = near_part + far_part + NUGGET * vectors
    gram_part = jnp.einsum("ip,jp->ij", all_columns, product, precision=EXACT_ARITHMETIC)
    gram_matrix = lax.psum(gram_part, "leaf") / (leaf_count * points_dev)
    return (product, gram_matrix)


def solution(mesh):
    return jax.shard_map(
        on_device,
        mesh=mesh,
        in_specs=(
            P("vec", "leaf"),
            P(None, "leaf"),
            P(None, "leaf"),
            P("leaf", None, None),
            P(),
            P("leaf"),
            P("leaf"),
            P("leaf"),
        ),
        out_specs=(P("vec", "leaf"), P(None, "vec")),
        check_vma=False,
    )
```

profile of v0, /device:TPU:0, one launch (start us, length us, event | category | flops | bytes accessed | tf_op | source)
XLA Modules:
  0.0 216.0 jit_solution(17568019953974837203)
XLA Ops:
  7.2 2.3 %fusion.55 = f32[32,8,32]{2,1,0:T(8,128)S(1)} fusion(f32[8,32,256]{2,0,1:T(8,128)} %bitcast.178, f32[4,32,8,256]{3,2,1,0:T(8,128)} %bitcast.175), kind=kOutput, calls=%fused_computation.110 | convolution fusion | flops 25165824 | bytes 1343488 | tf_op jit(solution)/shard_map/vlp,rlp->lvr/dot_general | solution.py:184
  11.4 4.9 %collective-permute-start.10 = (f32[2,8,32]{2,1,0:T(8,128)S(1)}, f32[2,8,32]{2,1,0:T(8,128)S(1)}, u32[]{:S(2)}, u32[]{:S(2)}) collective-permute-start(f32[2,8,32]{2,1,0:T(8,128)S(1)} %slice_add_fusion.3), channel_id=1, source_target_pairs={{0,4},{4,8},{8,12},{12,16},{16,20},{20,24},{24,28},{1,5},{5,9},{9,... | collective-permute-start | bytes 6152 | tf_op jit(solution)/shard_map/ppermute | solution.py:24
  18.3 5.1 %collective-permute-start.8 = (f32[3,8,32]{2,1,0:T(8,128)}, f32[3,8,32]{2,1,0:T(8,128)}, u32[]{:S(2)}, u32[]{:S(2)}) collective-permute-start(f32[3,8,32]{2,1,0:T(8,128)} %get-tuple-element.113), channel_id=1, source_target_pairs={{0,4},{4,8},{8,12},{12,16},{16,20},{20,24},{24,28},{1,5},{5,9},{9,... | collective-permute-start | bytes 9224 | tf_op jit(solution)/shard_map/ppermute | solution.py:24
  24.0 4.4 %collective-permute-start.6 = (f32[3,8,32]{2,1,0:T(8,128)}, f32[3,8,32]{2,1,0:T(8,128)}, u32[]{:S(2)}, u32[]{:S(2)}) collective-permute-start(f32[3,8,32]{2,1,0:T(8,128)} %get-tuple-element.111), channel_id=1, source_target_pairs={{0,4},{4,8},{8,12},{12,16},{16,20},{20,24},{24,28},{1,5},{5,9},{9,... | collective-permute-start | bytes 9224 | tf_op jit(solution)/shard_map/ppermute | solution.py:24
  29.9 31.5 %all_gather.7 = f32[8,8,32]{2,1,0:T(8,128)S(1)} all-gather(f32[1,8,32]{2,1,0:T(8,128)S(1)} %slice_add_fusion.4), channel_id=1, replica_groups=mesh['leaf'=8,'vec'=4] {'leaf'}, dimensions={0}, use_global_device_ids=true | all-gather | bytes 9216 | tf_op jit(solution)/shard_map/all_gather | solution.py:205
  84.9 4.6 %collective-permute-start = (f32[35,1024]{1,0:T(8,128)S(1)}, f32[35,1024]{1,0:T(8,128)S(1)}, u32[]{:S(2)}, u32[]{:S(2)}) collective-permute-start(f32[35,1024]{1,0:T(8,128)S(1)} %get-tuple-element.103), channel_id=1, source_target_pairs={{0,4},{4,8},{8,12},{12,16},{16,20},{20,24},{24,28},{1,5},{5,9},{9,... | collective-permute-start | bytes 430088 | tf_op jit(solution)/shard_map/ppermute | solution.py:24
  92.9 5.2 %collective-permute-start.2 = (f32[3,8,32]{2,1,0:T(8,128)}, f32[3,8,32]{2,1,0:T(8,128)S(1)}, u32[]{:S(2)}, u32[]{:S(2)}) collective-permute-start(f32[3,8,32]{2,1,0:T(8,128)} %get-tuple-element.105), channel_id=1, source_target_pairs={{0,4},{4,8},{8,12},{12,16},{16,20},{20,24},{24,28},{1,5},{5,9},{9,... | collective-permute-start | bytes 9224 | tf_op jit(solution)/shard_map/ppermute | solution.py:24
  101.8 53.4 %while.11 = (s32[]{:T(128)}, f32[32,32,256]{2,1,0:T(8,128)S(1)}, s32[8,5]{1,0:T(8,128)S(1)}, f32[35,40,256]{2,0,1:T(8,128)}, s32[8,5]{1,0:T(8,128)S(1)}, /*index...) while((s32[]{:T(128)}, f32[32,32,256]{2,1,0:T(8,128)S(1)}, ...), condition=%wide.region_1.2_spmd.clone, body=%wide.region_0.1_spmd.clone.sunk | while | flops 146720672 | bytes 3547571 | solution.py:148
  104.7 2.4 %fusion.205 = f32[5,32,256]{2,1,0:T(8,128)S(1)} fusion(f32[5,256]{1,0:T(8,128)S(1)} %bitcast.189, f32[5,256]{1,0:T(8,128)S(1)} %bitcast.192, f32[5,256]{1,0:T(8,128)S(1)} %bitcast.190, f32[5,256]{1,0:T(8,128)S(1)} %bitcast.193, f32[5,256]{1,0:T(8,128)S(1)} %bitcast.191, f32[5,256]{1,0:T(8,128)S(1)} %bitcast.194, ...), kind=kOutput, calls=%fused_computation.22.clone.1 | convolution fusion | flops 130416640 | bytes 376832 | tf_op jit(solution)/shard_map/while/body/eval_jaxpr/vbs,bts->bvt/dot_general | solution.py:130
  108.5 2.0 gather_fusion
  111.4 2.4 %fusion.205 = f32[5,32,256]{2,1,0:T(8,128)S(1)} fusion(f32[5,256]{1,0:T(8,128)S(1)} %bitcast.189, f32[5,256]{1,0:T(8,128)S(1)} %bitcast.192, f32[5,256]{1,0:T(8,128)S(1)} %bitcast.190, f32[5,256]{1,0:T(8,128)S(1)} %bitcast.193, f32[5,256]{1,0:T(8,128)S(1)} %bitcast.191, f32[5,256]{1,0:T(8,128)S(1)} %bitcast.194, ...), kind=kOutput, calls=%fused_computation.22.clone.1 | convolution fusion | flops 130416640 | bytes 376832 | tf_op jit(solution)/shard_map/while/body/eval_jaxpr/vbs,bts->bvt/dot_general | solution.py:130
  115.2 2.0 gather_fusion
  118.0 2.4 %fusion.205 = f32[5,32,256]{2,1,0:T(8,128)S(1)} fusion(f32[5,256]{1,0:T(8,128)S(1)} %bitcast.189, f32[5,256]{1,0:T(8,128)S(1)} %bitcast.192, f32[5,256]{1,0:T(8,128)S(1)} %bitcast.190, f32[5,256]{1,0:T(8,128)S(1)} %bitcast.193, f32[5,256]{1,0:T(8,128)S(1)} %bitcast.191, f32[5,256]{1,0:T(8,128)S(1)} %bitcast.194, ...), kind=kOutput, calls=%fused_computation.22.clone.1 | convolution fusion | flops 130416640 | bytes 376832 | tf_op jit(solution)/shard_map/while/body/eval_jaxpr/vbs,bts->bvt/dot_general | solution.py:130
  121.8 2.0 gather_fusion
  124.7 2.4 %fusion.205 = f32[5,32,256]{2,1,0:T(8,128)S(1)} fusion(f32[5,256]{1,0:T(8,128)S(1)} %bitcast.189, f32[5,256]{1,0:T(8,128)S(1)} %bitcast.192, f32[5,256]{1,0:T(8,128)S(1)} %bitcast.190, f32[5,256]{1,0:T(8,128)S(1)} %bitcast.193, f32[5,256]{1,0:T(8,128)S(1)} %bitcast.191, f32[5,256]{1,0:T(8,128)S(1)} %bitcast.194, ...), kind=kOutput, calls=%fused_computation.22.clone.1 | convolution fusion | flops 130416640 | bytes 376832 | tf_op jit(solution)/shard_map/while/body/eval_jaxpr/vbs,bts->bvt/dot_general | solution.py:130
  128.5 2.0 gather_fusion
  131.4 2.4 %fusion.205 = f32[5,32,256]{2,1,0:T(8,128)S(1)} fusion(f32[5,256]{1,0:T(8,128)S(1)} %bitcast.189, f32[5,256]{1,0:T(8,128)S(1)} %bitcast.192, f32[5,256]{1,0:T(8,128)S(1)} %bitcast.190, f32[5,256]{1,0:T(8,128)S(1)} %bitcast.193, f32[5,256]{1,0:T(8,128)S(1)} %bitcast.191, f32[5,256]{1,0:T(8,128)S(1)} %bitcast.194, ...), kind=kOutput, calls=%fused_computation.22.clone.1 | convolution fusion | flops 130416640 | bytes 376832 | tf_op jit(solution)/shard_map/while/body/eval_jaxpr/vbs,bts->bvt/dot_general | solution.py:130
  138.1 2.4 %fusion.205 = f32[5,32,256]{2,1,0:T(8,128)S(1)} fusion(f32[5,256]{1,0:T(8,128)S(1)} %bitcast.189, f32[5,256]{1,0:T(8,128)S(1)} %bitcast.192, f32[5,256]{1,0:T(8,128)S(1)} %bitcast.190, f32[5,256]{1,0:T(8,128)S(1)} %bitcast.193, f32[5,256]{1,0:T(8,128)S(1)} %bitcast.191, f32[5,256]{1,0:T(8,128)S(1)} %bitcast.194, ...), kind=kOutput, calls=%fused_computation.22.clone.1 | convolution fusion | flops 130416640 | bytes 376832 | tf_op jit(solution)/shard_map/while/body/eval_jaxpr/vbs,bts->bvt/dot_general | solution.py:130
  144.7 2.4 %fusion.205 = f32[5,32,256]{2,1,0:T(8,128)S(1)} fusion(f32[5,256]{1,0:T(8,128)S(1)} %bitcast.189, f32[5,256]{1,0:T(8,128)S(1)} %bitcast.192, f32[5,256]{1,0:T(8,128)S(1)} %bitcast.190, f32[5,256]{1,0:T(8,128)S(1)} %bitcast.193, f32[5,256]{1,0:T(8,128)S(1)} %bitcast.191, f32[5,256]{1,0:T(8,128)S(1)} %bitcast.194, ...), kind=kOutput, calls=%fused_computation.22.clone.1 | convolution fusion | flops 130416640 | bytes 376832 | tf_op jit(solution)/shard_map/while/body/eval_jaxpr/vbs,bts->bvt/dot_general | solution.py:130
  148.6 2.0 gather_fusion
  151.4 2.4 %fusion.205 = f32[5,32,256]{2,1,0:T(8,128)S(1)} fusion(f32[5,256]{1,0:T(8,128)S(1)} %bitcast.189, f32[5,256]{1,0:T(8,128)S(1)} %bitcast.192, f32[5,256]{1,0:T(8,128)S(1)} %bitcast.190, f32[5,256]{1,0:T(8,128)S(1)} %bitcast.193, f32[5,256]{1,0:T(8,128)S(1)} %bitcast.191, f32[5,256]{1,0:T(8,128)S(1)} %bitcast.194, ...), kind=kOutput, calls=%fused_computation.22.clone.1 | convolution fusion | flops 130416640 | bytes 376832 | tf_op jit(solution)/shard_map/while/body/eval_jaxpr/vbs,bts->bvt/dot_general | solution.py:130
  174.8 3.2 %fusion.46 = f32[32,8,32]{2,1,0:T(8,128)S(1)} fusion(f32[32,32,3,32]{3,2,1,0:T(4,128)S(1)} %copy-done.1, f32[32,1,8,32]{3,2,0,1:T(8,128)S(1)} %bitcast.181, f32[32,1,8,32]{3,2,0,1:T(8,128)S(1)} %bitcast.180, f32[32,1,8,32]{3,2,0,1:T(8,128)} %bitcast.182), kind=kOutput, calls=%fused_computation.89 | convolution fusion | flops 9486336 | bytes 524288 | tf_op jit(solution)/shard_map/navr,nras->nvs/dot_general | solution.py:55
  182.2 3.1 %reduce-scatter.2.cloned.1.call-done = f32[8,8192]{1,0:T(8,128)} async-done(((f32[32,8192]{1,0:T(8,128)}), f32[8,8192]{1,0:T(8,128)}) %reduce-scatter.2.cloned.1.call-update) | async-done | bytes 262160 | tf_op jit(solution)/shard_map/reduce_scatter | solution.py:182
  187.2 21.4 %psum.7 = f32[32,8]{0,1:T(8,128)S(1)} all-reduce(f32[32,8]{0,1:T(8,128)S(1)} %convolution_bitcast_fusion.5), channel_id=1, replica_groups=mesh['leaf'=8,'vec'=4] {'leaf'}, use_global_device_ids=true, to_apply=%region_3.4 | all-reduce | flops 256 | bytes 2048 | tf_op jit(solution)/shard_map/psum | solution.py:228
  (325 shorter events, 84.6 us)
Async XLA Ops:
  7.2 76.3 %all-gather.2.cloned.1.call-start = ((), (), s32[]{:S(2)}) async-start(), calls=%async_computation.1 | async-start | bytes 1310720 | tf_op jit(solution)/shard_map/all_gather | solution.py:161
  10.3 56.1 %copy-start.21 = (s32[4]{0:T(128)S(1)}, s32[4]{0:T(128)}, u32[]{:S(2)}) copy-start(s32[4]{0:T(128)} %constant.215) | copy-start | bytes 52
  10.3 56.1 %copy-start.22 = (s32[4]{0:T(128)S(1)}, s32[4]{0:T(128)}, u32[]{:S(2)}) copy-start(s32[4]{0:T(128)} %constant.216) | copy-start | bytes 52
  10.3 56.7 %copy-start.19 = (s32[8]{0:T(128)S(1)}, s32[8]{0:T(128)}, u32[]{:S(2)}) copy-start(s32[8]{0:T(128)} %constant.212) | copy-start | bytes 100
  10.3 56.7 %copy-start.20 = (s32[8]{0:T(128)S(1)}, s32[8]{0:T(128)}, u32[]{:S(2)}) copy-start(s32[8]{0:T(128)} %constant.213) | copy-start | bytes 100
  10.3 57.3 %copy-start.17 = (s32[16]{0:T(128)S(1)}, s32[16]{0:T(128)}, u32[]{:S(2)}) copy-start(s32[16]{0:T(128)} %constant.209) | copy-start | bytes 196
  10.3 57.3 %copy-start.18 = (s32[16]{0:T(128)S(1)}, s32[16]{0:T(128)}, u32[]{:S(2)}) copy-start(s32[16]{0:T(128)} %constant.210) | copy-start | bytes 196
  10.4 57.9 %copy-start.15 = (s32[32]{0:T(128)S(1)}, s32[32]{0:T(128)}, u32[]{:S(2)}) copy-start(s32[32]{0:T(128)} %constant.206) | copy-start | bytes 388
  10.4 57.9 %copy-start.16 = (s32[32]{0:T(128)S(1)}, s32[32]{0:T(128)}, u32[]{:S(2)}) copy-start(s32[32]{0:T(128)} %constant.207) | copy-start | bytes 388
  10.4 58.5 %copy-start.13 = (s32[160]{0:T(256)S(1)}, s32[160]{0:T(256)}, u32[]{:S(2)}) copy-start(s32[160]{0:T(256)} %param.46) | copy-start | bytes 1924
  10.4 58.5 %copy-start.14 = (s32[160]{0:T(256)S(1)}, s32[160]{0:T(256)}, u32[]{:S(2)}) copy-start(s32[160]{0:T(256)} %param.45) | copy-start | bytes 1924
  11.4 67.0 %collective-permute-start.10 = (f32[2,8,32]{2,1,0:T(8,128)S(1)}, f32[2,8,32]{2,1,0:T(8,128)S(1)}, u32[]{:S(2)}, u32[]{:S(2)}) collective-permute-start(f32[2,8,32]{2,1,0:T(8,128)S(1)} %slice_add_fusion.3), channel_id=1, source_target_pairs={{0,4},{4,8},{8,12},{12,16},{16,20},{20,24},{24,28},{1,5},{5,9},{9,... | collective-permute-start | bytes 6152 | tf_op jit(solution)/shard_map/ppermute | solution.py:24
  16.3 63.7 %collective-permute-start.11 = (f32[2,8,32]{2,1,0:T(8,128)S(1)}, f32[2,8,32]{2,1,0:T(8,128)S(1)}, u32[]{:S(2)}, u32[]{:S(2)}) collective-permute-start(f32[2,8,32]{2,1,0:T(8,128)S(1)} %slice_add_fusion.3), channel_id=1, source_target_pairs={{4,0},{8,4},{12,8},{16,12},{20,16},{24,20},{28,24},{5,1},{9,5},{13... | collective-permute-start | bytes 6152 | tf_op jit(solution)/shard_map/ppermute | solution.py:27
  17.6 167.6 %reduce-scatter.2.cloned.1.call-start = ((), (), s32[]{:S(2)}) async-start(), calls=%async_computation.2 | async-start | bytes 1310720 | tf_op jit(solution)/shard_map/reduce_scatter | solution.py:182
  18.3 138.5 %collective-permute-start.8 = (f32[3,8,32]{2,1,0:T(8,128)}, f32[3,8,32]{2,1,0:T(8,128)}, u32[]{:S(2)}, u32[]{:S(2)}) collective-permute-start(f32[3,8,32]{2,1,0:T(8,128)} %get-tuple-element.113), channel_id=1, source_target_pairs={{0,4},{4,8},{8,12},{12,16},{16,20},{20,24},{24,28},{1,5},{5,9},{9,... | collective-permute-start | bytes 9224 | tf_op jit(solution)/shard_map/ppermute | solution.py:24
  24.0 60.9 %collective-permute-start.6 = (f32[3,8,32]{2,1,0:T(8,128)}, f32[3,8,32]{2,1,0:T(8,128)}, u32[]{:S(2)}, u32[]{:S(2)}) collective-permute-start(f32[3,8,32]{2,1,0:T(8,128)} %get-tuple-element.111), channel_id=1, source_target_pairs={{0,4},{4,8},{8,12},{12,16},{16,20},{20,24},{24,28},{1,5},{5,9},{9,... | collective-permute-start | bytes 9224 | tf_op jit(solution)/shard_map/ppermute | solution.py:24
  28.4 61.1 %collective-permute-start.7 = (f32[3,8,32]{2,1,0:T(8,128)}, f32[3,8,32]{2,1,0:T(8,128)}, u32[]{:S(2)}, u32[]{:S(2)}) collective-permute-start(f32[3,8,32]{2,1,0:T(8,128)} %get-tuple-element.112), channel_id=1, source_target_pairs={{4,0},{8,4},{12,8},{16,12},{20,16},{24,20},{28,24},{5,1},{9,5},{13... | collective-permute-start | bytes 9224 | tf_op jit(solution)/shard_map/ppermute | solution.py:27
  78.4 13.2 %collective-permute-start.4 = (f32[3,8,32]{2,1,0:T(8,128)}, f32[3,8,32]{2,1,0:T(8,128)S(1)}, u32[]{:S(2)}, u32[]{:S(2)}) collective-permute-start(f32[3,8,32]{2,1,0:T(8,128)} %get-tuple-element.107), channel_id=1, source_target_pairs={{0,4},{4,8},{8,12},{12,16},{16,20},{20,24},{24,28},{1,5},{5,9},{9,... | collective-permute-start | bytes 9224 | tf_op jit(solution)/shard_map/ppermute | solution.py:24
  80.0 12.9 %collective-permute-start.5 = (f32[3,8,32]{2,1,0:T(8,128)}, f32[3,8,32]{2,1,0:T(8,128)S(1)}, u32[]{:S(2)}, u32[]{:S(2)}) collective-permute-start(f32[3,8,32]{2,1,0:T(8,128)} %get-tuple-element.108), channel_id=1, source_target_pairs={{4,0},{8,4},{12,8},{16,12},{20,16},{24,20},{28,24},{5,1},{9,5},{13... | collective-permute-start | bytes 9224 | tf_op jit(solution)/shard_map/ppermute | solution.py:27
  84.9 13.1 %collective-permute-start = (f32[35,1024]{1,0:T(8,128)S(1)}, f32[35,1024]{1,0:T(8,128)S(1)}, u32[]{:S(2)}, u32[]{:S(2)}) collective-permute-start(f32[35,1024]{1,0:T(8,128)S(1)} %get-tuple-element.103), channel_id=1, source_target_pairs={{0,4},{4,8},{8,12},{12,16},{16,20},{20,24},{24,28},{1,5},{5,9},{9,... | collective-permute-start | bytes 430088 | tf_op jit(solution)/shard_map/ppermute | solution.py:24
  89.5 9.9 %collective-permute-start.1 = (f32[35,1024]{1,0:T(8,128)S(1)}, f32[35,1024]{1,0:T(8,128)S(1)}, u32[]{:S(2)}, u32[]{:S(2)}) collective-permute-start(f32[35,1024]{1,0:T(8,128)S(1)} %get-tuple-element.104), channel_id=1, source_target_pairs={{4,0},{8,4},{12,8},{16,12},{20,16},{24,20},{28,24},{5,1},{9,5},{13... | collective-permute-start | bytes 430088 | tf_op jit(solution)/shard_map/ppermute | solution.py:27
  91.6 65.3 %collective-permute-start.9 = (f32[3,8,32]{2,1,0:T(8,128)S(1)}, f32[3,8,32]{2,1,0:T(8,128)S(1)}, u32[]{:S(2)}, u32[]{:S(2)}) collective-permute-start(f32[3,8,32]{2,1,0:T(8,128)S(1)} %copy-done.12), channel_id=1, source_target_pairs={{4,0},{8,4},{12,8},{16,12},{20,16},{24,20},{28,24},{5,1},{9,5},{13... | collective-permute-start | bytes 9224 | tf_op jit(solution)/shard_map/ppermute | solution.py:27
  92.9 75.9 %collective-permute-start.2 = (f32[3,8,32]{2,1,0:T(8,128)}, f32[3,8,32]{2,1,0:T(8,128)S(1)}, u32[]{:S(2)}, u32[]{:S(2)}) collective-permute-start(f32[3,8,32]{2,1,0:T(8,128)} %get-tuple-element.105), channel_id=1, source_target_pairs={{0,4},{4,8},{8,12},{12,16},{16,20},{20,24},{24,28},{1,5},{5,9},{9,... | collective-permute-start | bytes 9224 | tf_op jit(solution)/shard_map/ppermute | solution.py:24
  98.1 70.6 %collective-permute-start.3 = (f32[3,8,32]{2,1,0:T(8,128)}, f32[3,8,32]{2,1,0:T(8,128)S(1)}, u32[]{:S(2)}, u32[]{:S(2)}) collective-permute-start(f32[3,8,32]{2,1,0:T(8,128)} %get-tuple-element.106), channel_id=1, source_target_pairs={{4,0},{8,4},{12,8},{16,12},{20,16},{24,20},{28,24},{5,1},{9,5},{13... | collective-permute-start | bytes 9224 | tf_op jit(solution)/shard_map/ppermute | solution.py:27
  (18 other events, 413.4 us)
Sparse Core Ops, SparseCore 0:
  17.8 19.0 all-gather.1
  157.0 28.2 reduce-scatter.1
where the time goes:
time: 217 us; the launch traced here: 216 us
  blocking collectives  52.8 us (24%)
  local copies, waits for them, and re-layouts  52.2 us (24%)
  matrix products  48 us (22%)
  starting transfers between devices  33.5 us (15%)
  between operations  15.5 us (7%)
  other arithmetic  9.62 us (4%)
  waiting for transfers between devices  3.15 us (1%)
    all_gather x1, blocking collectives, on_device(): all_roots = lax.all_gather(current, 'leaf', axis=0, tiled=True)  31.5 us
    ppermute x6, starting transfers between devices, padded_2(): lax.ppermute(lax.slice_in_dim(block, block.shape[dim] - width, None, axis...  25.7 us
    psum x1, blocking collectives, on_device(): gram_matrix = lax.psum(gram_part, 'leaf') / (leaf_count * points_dev)  21.4 us
    dot_general x8, matrix products, add_block(): jnp.einsum('vbs,bts->bvt', source_rows[:columns], kernel, precision=EXACT...  19.2 us
    gather x8, local copies, waits for them, and re-layouts, add_block(): source_rows = jnp.take(window, source_ids, axis=1)  15.9 us
    gather x15, local copies, waits for them, and re-layouts, take_rows(): gathered.append(padded[np.arange(count_nodes) + shift_by + pad_width])  15.6 us
    dot_general x8, matrix products, add_block(): jnp.einsum('qs,qhg->hsg', selection_mask, contribution, precision=EXACT_A...  10.5 us
    dot_general x5, matrix products, couple_level(): jnp.einsum('navr,nras->nvs', sources, blocks, precision=EXACT_ARITHMETIC)  7.84 us
  transfers between devices with their start and end apart: 14, of which 1 were waited for; matrix products, arithmetic and copies ran while one was open for 48% of the time, Pallas kernels for 0%

commit v1 on v0

v1 whole, which is shorter than its diff:
```python
import functools

import jax
import jax.numpy as jnp
from jax import lax
from jax.experimental import pallas as pl
from jax.experimental.pallas import tpu as pltpu
from jax.sharding import PartitionSpec as P

PTS = 256
REACH = 4
SIGNAL = 0.1
NUGGET = 0.5
LENGTH = 0.35
SLAB = 0.25
SCALE = 3.0 ** 0.5 / LENGTH
MESH = pl.DeviceIdType.MESH
F32 = jnp.float32
BF16 = jnp.bfloat16
LANES = 128


def halves(x):
    high = x.astype(BF16)
    return high, (x - high.astype(F32)).astype(BF16)


def dot3(a, b, dims):
    ah, al = halves(a)
    bh, bl = halves(b)

    def one(x, y):
        return lax.dot_general(x, y, (dims, ((), ())), preferred_element_type=F32)

    return one(ah, bh) + (one(al, bh) + one(ah, bl))


NN = ((1,), (0,))
NT = ((1,), (1,))


def kernel(cfg, offs, wts, vecs, coords, basis, ops, tops, out, gram, *scr):
    D, V, LD, RK, rounds, toplev = cfg
    cols = vecs.shape[0]
    NC = cols * V
    L = LD // V
    C = L * PTS
    H = REACH * PTS
    PD = LD * PTS
    (win, vhl, crd, bcol, basis_v, ops_v, tops_v, kh, kl, prod, lev, up, roots, fld, gsend, gpart, gall) = scr[:17]
    (s_loc, s_vec, r_vec, s_x, r_x, s_c, r_c, s_e, r_e, s_u, r_u, s_h, r_h, s_r, r_r, s_o, r_o, s_g, r_g, s_q, r_q) = scr[17:]
    d = lax.axis_index("leaf")
    v = lax.axis_index("vec")
    g = d * V + v
    has_left = g > 0
    has_right = g < D * V - 1

    local_levels = []
    n, base, row = L, 0, 0
    while n >= 2:
        local_levels.append((n, base, row))
        base += n + 4
        row += LD // L * n
        n //= 2
    up_levels = []
    n, base = V, 0
    while n >= 2:
        up_levels.append((n, base, row))
        base += n + 4
        row += n
        n //= 2

    own = pl.ds(v * cols, cols)
    chunk = pl.ds(pl.multiple_of(v * C, C), C)
    loads = [
        pltpu.make_async_copy(vecs.at[:, chunk], win.at[own, pl.ds(H, C)], s_loc.at[0]),
        pltpu.make_async_copy(coords.at[:, chunk], crd.at[:, pl.ds(H, C)], s_loc.at[1]),
        pltpu.make_async_copy(basis.at[:, chunk], basis_v, s_loc.at[2]),
        pltpu.make_async_copy(ops, ops_v, s_loc.at[3]),
        pltpu.make_async_copy(tops, tops_v, s_loc.at[4]),
    ]
    for copy in loads:
        copy.start()
    low_from = pl.ds(pl.multiple_of(jnp.maximum(v * C - H, 0), H), H)
    high_from = pl.ds(pl.multiple_of(jnp.minimum(v * C + C, PD - H), H), H)
    low_loads = [
        pltpu.make_async_copy(vecs.at[:, low_from], win.at[own, pl.ds(0, H)], s_loc.at[5]),
        pltpu.make_async_copy(coords.at[:, low_from], crd.at[:, pl.ds(0, H)], s_loc.at[6]),
    ]
    high_loads = [
        pltpu.make_async_copy(vecs.at[:, high_from], win.at[own, pl.ds(H + C, H)], s_loc.at[7]),
        pltpu.make_async_copy(coords.at[:, high_from], crd.at[:, pl.ds(H + C, H)], s_loc.at[8]),
    ]

    @pl.when(v > 0)
    def _():
        for copy in low_loads:
            copy.start()

    @pl.when(v < V - 1)
    def _():
        for copy in high_loads:
            copy.start()

    barrier = pltpu.get_barrier_semaphore()
    for k in range(1, V):
        pl.semaphore_signal(barrier, inc=1, device_id=(d, lax.rem(v + k, V)), device_id_type=MESH)
    for k in range(1, D):
        pl.semaphore_signal(barrier, inc=1, device_id=(lax.rem(d + k, D), v), device_id_type=MESH)

    @pl.when(d > 0)
    def _():
        for k in range(1, V):
            pl.semaphore_signal(barrier, inc=1, device_id=(d - 1, lax.rem(v + k, V)), device_id_type=MESH)

    @pl.when(d < D - 1)
    def _():
        for k in range(1, V):
            pl.semaphore_signal(barrier, inc=1, device_id=(d + 1, lax.rem(v + k, V)), device_id_type=MESH)

    sides = (d > 0).astype(jnp.int32) + (d < D - 1).astype(jnp.int32)
    pl.semaphore_wait(barrier, V - 1 + D - 1 + (V - 1) * sides)

    def remote(src, dst, ss, rs, where):
        return pltpu.make_async_remote_copy(
            src_ref=src, dst_ref=dst, send_sem=ss, recv_sem=rs, device_id=where, device_id_type=MESH
        )

    def vec_copies(t):
        parts = [(0, t * C, H, C)]
        if t > 0:
            parts.append((1, t * C - H, 0, H))
        if t < V - 1:
            parts.append((2, t * C + C, H + C, H))
        return [
            remote(
                vecs.at[:, pl.ds(src, size)],
                win.at[own, pl.ds(dst, size)],
                s_vec.at[k, t],
                r_vec.at[k, v],
                (d, t),
            )
            for k, src, dst, size in parts
        ]

    cross_right = remote(
        vecs.at[:, pl.ds(PD - H, H)], win.at[own, pl.ds(0, H)], s_x.at[0], r_x.at[0, v], (jnp.minimum(d + 1, D - 1), 0)
    )
    cross_left = remote(
        vecs.at[:, pl.ds(0, H)], win.at[own, pl.ds(H + C, H)], s_x.at[1], r_x.at[1, v], (jnp.maximum(d - 1, 0), V - 1)
    )
    crd_right = remote(
        coords.at[:, pl.ds(PD - H, H)], crd.at[:, pl.ds(0, H)], s_c.at[0], r_c.at[0], (jnp.minimum(d + 1, D - 1), 0)
    )
    crd_left = remote(
        coords.at[:, pl.ds(0, H)], crd.at[:, pl.ds(H + C, H)], s_c.at[1], r_c.at[1], (jnp.maximum(d - 1, 0), V - 1)
    )
    for t in range(V):

        @pl.when(v != t)
        def _(t=t):
            for copy in vec_copies(t):
                copy.start()

    @pl.when(d < D - 1)
    def _():
        cross_right.start()

        @pl.when(v == V - 1)
        def _():
            crd_right.start()

    @pl.when(d > 0)
    def _():
        cross_left.start()

        @pl.when(v == 0)
        def _():
            crd_left.start()

    def zero_nodes(ref, lo, size):
        ref[lo : lo + size] = jnp.zeros((size,) + ref.shape[1:], F32)

    @pl.when(jnp.logical_not(has_left))
    def _():
        win[:, 0:H] = jnp.zeros((NC, H), F32)
        crd[:, 0:H] = jnp.zeros((crd.shape[0], H), F32)
        for n, base, row in local_levels:
            zero_nodes(lev, base, 2)

    @pl.when(jnp.logical_not(has_right))
    def _():
        win[:, H + C :] = jnp.zeros((NC, H), F32)
        crd[:, H + C :] = jnp.zeros((crd.shape[0], H), F32)
        for n, base, row in local_levels:
            zero_nodes(lev, base + 2 + n, 2)

    @pl.when(d == 0)
    def _():
        for n, base, row in up_levels:
            zero_nodes(up, base, 2)

    @pl.when(d == D - 1)
    def _():
        for n, base, row in up_levels:
            zero_nodes(up, base + 2 + n, 2)

    root_base = []
    base = 0
    for k in range(toplev):
        size = D >> k
        zero_nodes(roots, base, 3)
        zero_nodes(roots, base + 3 + size, 3)
        root_base.append(base)
        base += size + 6

    def arrived(dst, rs):
        return pltpu.make_async_copy(dst, dst, rs)

    for copy in loads:
        copy.wait()

    @pl.when(v > 0)
    def _():
        for copy in low_loads:
            copy.wait()

    @pl.when(v < V - 1)
    def _():
        for copy in high_loads:
            copy.wait()

    for s in range(V):
        rows = pl.ds(s * cols, cols)

        @pl.when(v != s)
        def _(s=s, rows=rows):
            arrived(win.at[rows, pl.ds(H, C)], r_vec.at[0, s]).wait()

    def op(i):
        return ops_v[i]

    def coef(ref, i):
        return ref[i][:, :RK]

    def raised(ref, i, row):
        both = dot3(coef(ref, i), op(row), NN) + dot3(coef(ref, i + 1), op(row + 1), NN)
        return pltpu.roll(both, RK, 1)

    for l in range(L):
        points = slice(l * PTS, (l + 1) * PTS)
        lev[2 + l, :, :RK] = dot3(win[:, H + l * PTS : H + (l + 1) * PTS], basis_v[:, points], NT)
    for index, (n, base, row) in enumerate(local_levels):
        for q in range(n // 2):
            value = raised(lev, base + 2 + 2 * q, row + v * n + 2 * q)
            if index + 1 < len(local_levels):
                lev[local_levels[index + 1][1] + 2 + q] = value
            else:
                up[2 + v] = value

    def edge_copies(side, where):
        copies = []
        for k, (n, base, row) in enumerate(local_levels):
            src = base + 2 if side == 0 else base + n
            dst = base + 2 + n if side == 0 else base
            copies.append(
                remote(lev.at[pl.ds(src, 2)], lev.at[pl.ds(dst, 2)], s_e.at[side, k], r_e.at[side, k], where)
            )
        return copies

    left_id = (jnp.maximum(g - 1, 0) // V, lax.rem(jnp.maximum(g - 1, 0), V))
    right_id = (jnp.minimum(g + 1, D * V - 1) // V, lax.rem(jnp.minimum(g + 1, D * V - 1), V))
    edges_left = edge_copies(0, left_id)
    edges_right = edge_copies(1, right_id)

    @pl.when(has_left)
    def _():
        for copy in edges_left:
            copy.start()

    @pl.when(has_right)
    def _():
        for copy in edges_right:
            copy.start()

    up_copies = [
        remote(up.at[2 + v], up.at[2 + v], s_u.at[k], r_u.at[v], (d, lax.rem(v + k, V))) for k in range(1, V)
    ]
    for copy in up_copies:
        copy.start()

    for s in range(V):
        rows = pl.ds(s * cols, cols)

        @pl.when(jnp.logical_and(v > 0, v != s))
        def _(s=s, rows=rows):
            arrived(win.at[rows, pl.ds(0, H)], r_vec.at[1, s]).wait()

        @pl.when(jnp.logical_and(v < V - 1, v != s))
        def _(s=s, rows=rows):
            arrived(win.at[rows, pl.ds(H + C, H)], r_vec.at[2, s]).wait()

        @pl.when(jnp.logical_and(v == 0, d > 0))
        def _(s=s, rows=rows):
            arrived(win.at[rows, pl.ds(0, H)], r_x.at[0, s]).wait()

        @pl.when(jnp.logical_and(v == V - 1, d < D - 1))
        def _(s=s, rows=rows):
            arrived(win.at[rows, pl.ds(H + C, H)], r_x.at[1, s]).wait()

    @pl.when(jnp.logical_and(v == 0, d > 0))
    def _():
        arrived(crd.at[:, pl.ds(0, H)], r_c.at[0]).wait()

    @pl.when(jnp.logical_and(v == V - 1, d < D - 1))
    def _():
        arrived(crd.at[:, pl.ds(H + C, H)], r_c.at[1]).wait()

    origin = (g * L).astype(F32) * SLAB
    first = lax.broadcasted_iota(jnp.int32, crd.shape, 0) == 0
    crd[...] = (crd[...] - jnp.where(first, origin, 0.0)) * SCALE

    def spread(i, carry):
        at = pl.ds(pl.multiple_of(i * LANES, LANES), LANES)
        tall = crd[:, at].T
        for axis in range(3):
            bcol[i // 2, axis, pl.ds(pl.multiple_of(lax.rem(i, 2) * LANES, LANES), LANES), :] = jnp.broadcast_to(
                tall[:, axis : axis + 1], (LANES, LANES)
            )
        return carry

    lax.fori_loop(0, (C + 2 * H) // LANES, spread, 0)

    for leaf in range(L + 2 * REACH):
        high, low = halves(win[:, leaf * PTS : (leaf + 1) * PTS])
        vhl[leaf, :NC] = high
        vhl[leaf, NC:] = low

    step = 64

    def near(t, carry):
        here = pl.ds(pl.multiple_of(H + t * PTS, PTS), PTS)
        target = [crd[axis : axis + 1, here] for axis in range(3)]
        total = jnp.zeros((NC, PTS), F32)
        for r in range(rounds):
            slot = r * LD + v * L + t
            source = bcol[offs[slot]]
            for sub in range(PTS // step):
                rows = slice(sub * step, (sub + 1) * step)
                for half in range(PTS // LANES):
                    lanes = slice(half * LANES, (half + 1) * LANES)
                    dist = None
                    for axis in range(3):
                        gap = source[axis, rows] - target[axis][:, lanes]
                        dist = gap * gap if dist is None else dist + gap * gap
                    u = dist * lax.rsqrt(jnp.maximum(dist, 1e-30))
                    block = (1.0 + u) * jnp.exp(-u)
                    high, low = halves(block)
                    kh[r, rows, lanes] = high
                    kl[r, rows, lanes] = low
            moved = vhl[offs[slot]]
            both = jnp.dot(moved, kh[r], preferred_element_type=F32)
            small = jnp.dot(moved[:NC], kl[r], preferred_element_type=F32)
            total = total + ((both[:NC] + both[NC:]) + small) * wts[slot]
        prod[:, pl.ds(pl.multiple_of(t * PTS, PTS), PTS)] = total
        return carry

    cut = L // 2
    lax.fori_loop(0, cut, near, 0)

    for s in range(V):

        @pl.when(v != s)
        def _(s=s):
            arrived(up.at[2 + s], r_u.at[s]).wait()

    for copy in up_copies:
        copy.wait_send()
    for index, (n, base, row) in enumerate(up_levels):
        for q in range(n // 2):
            value = raised(up, base + 2 + 2 * q, row + 2 * q)
            if index + 1 < len(up_levels):
                up[up_levels[index + 1][1] + 2 + q] = value
            else:
                roots[3 + d] = value

    def halo_copies(side, where):
        copies = []
        for k, (n, base, row) in enumerate(up_levels):
            src = base + 2 if side == 0 else base + n
            dst = base + 2 + n if side == 0 else base
            copies.append(
                remote(up.at[pl.ds(src, 2)], up.at[pl.ds(dst, 2)], s_h.at[side, k], r_h.at[side, k], where)
            )
        return copies

    halos_left = halo_copies(0, (jnp.maximum(d - 1, 0), v))
    halos_right = halo_copies(1, (jnp.minimum(d + 1, D - 1), v))

    @pl.when(d > 0)
    def _():
        for copy in halos_left:
            copy.start()

    @pl.when(d < D - 1)
    def _():
        for copy in halos_right:
            copy.start()

    root_copies = [
        remote(roots.at[3 + d], roots.at[3 + d], s_r.at[k], r_r.at[d], (lax.rem(d + k, D), v)) for k in range(1, D)
    ]
    for copy in root_copies:
        copy.start()

    lax.fori_loop(cut, L, near, 0)

    for s in range(D):

        @pl.when(d != s)
        def _(s=s):
            arrived(roots.at[3 + s], r_r.at[s]).wait()

    for copy in root_copies:
        copy.wait_send()

    @pl.when(d > 0)
    def _():
        for copy in halos_left:
            copy.wait_send()
        for k, (n, base, row) in enumerate(up_levels):
            arrived(up.at[pl.ds(base, 2)], r_h.at[1, k]).wait()

    @pl.when(d < D - 1)
    def _():
        for copy in halos_right:
            copy.wait_send()
        for k, (n, base, row) in enumerate(up_levels):
            arrived(up.at[pl.ds(base + 2 + n, 2)], r_h.at[0, k]).wait()

    @pl.when(has_left)
    def _():
        for copy in edges_left:
            copy.wait_send()
        for k, (n, base, row) in enumerate(local_levels):
            arrived(lev.at[pl.ds(base, 2)], r_e.at[1, k]).wait()

    @pl.when(has_right)
    def _():
        for copy in edges_right:
            copy.wait_send()
        for k, (n, base, row) in enumerate(local_levels):
            arrived(lev.at[pl.ds(base + 2 + n, 2)], r_e.at[0, k]).wait()

    top_fields = []
    for k in range(toplev):
        base, size = root_base[k], D >> k
        node = d // (1 << k)
        odd = lax.rem(node, 2).astype(F32)
        weights = (odd, 1.0, 1.0, 1.0 - odd)
        table = tops_v[k]
        partners = jnp.concatenate([coef(roots, base + 3 + node + o) for o in (-3, -2, 2, 3)], axis=0)
        moved = dot3(partners, table[:, : 4 * RK], NN)
        total = moved[:RK * 0 + NC] * weights[0]
        for j in range(1, 4):
            total = total + pltpu.roll(moved[j * NC : (j + 1) * NC], LANES - j * RK, 1) * weights[j]
        top_fields.append(total[:, :RK])
        if k + 1 < toplev:
            for q in range(size // 2):
                value = dot3(coef(roots, base + 3 + 2 * q), table[:, 4 * RK : 5 * RK], NN) + dot3(
                    coef(roots, base + 4 + 2 * q), table[:, 5 * RK :], NN
                )
                roots[root_base[k + 1] + 3 + q, :, :RK] = value
    down = top_fields[toplev - 1]
    for k in range(toplev - 2, -1, -1):
        odd = lax.rem(d // (1 << k), 2).astype(F32)
        table = tops_v[k]
        even_part = dot3(down, table[:, 4 * RK : 5 * RK], NT)
        odd_part = dot3(down, table[:, 5 * RK :], NT)
        down = top_fields[k] + even_part * (1.0 - odd) + odd_part * odd

    def coupled(ref, sources, row):
        moved = dot3(jnp.concatenate([coef(ref, i) for i in sources], axis=0), op(row), NN)
        return (
            moved[:NC]
            + pltpu.roll(moved[NC : 2 * NC], LANES - RK, 1)
            + pltpu.roll(moved[2 * NC :], LANES - 2 * RK, 1)
        )[:, :RK]

    def lowered(parent, row):
        zeros = jnp.zeros((NC, 3 * RK), F32)
        return dot3(jnp.concatenate([zeros, parent], axis=1), op(row), NT)

    for index in range(len(up_levels) - 1, -1, -1):
        n, base, row = up_levels[index]
        node = v // (V // n)
        odd = lax.rem(node, 2)
        at = base + 2 + node
        sources = (at - 2 - odd, at + 2 - 4 * odd, at + 3 - odd)
        down = coupled(up, sources, row + node) + lowered(down, row + node)
    downs = [down]
    for index in range(len(local_levels) - 1, -1, -1):
        n, base, row = local_levels[index]
        fresh = []
        for i in range(n):
            shifts = (-2, 2, 3) if i % 2 == 0 else (-3, -2, 2)
            sources = [base + 2 + i + o for o in shifts]
            where = row + v * n + i
            fresh.append(coupled(lev, sources, where) + lowered(downs[i // 2], where))
        downs = fresh

    inner = jnp.zeros((NC, NC), F32)
    for l in range(L):
        points = slice(l * PTS, (l + 1) * PTS)
        mine = win[:, H + l * PTS : H + (l + 1) * PTS]
        value = prod[:, points] + dot3(downs[l], basis_v[:, points], NN) + NUGGET * mine
        prod[:, points] = value
        inner = inner + dot3(value, mine, NT)
    for t in range(V):
        gsend[t, :, :NC] = inner[t * cols : (t + 1) * cols]

    def home(t):
        return remote(
            prod.at[pl.ds(t * cols, cols), :], out.at[:, chunk], s_o.at[t], r_o.at[v], (d, t)
        )

    def inner_copy(t):
        return remote(gsend.at[t], gpart.at[v], s_g.at[t], r_g.at[v], (d, t))

    for t in range(V):

        @pl.when(v != t)
        def _(t=t):
            inner_copy(t).start()

    stay = pltpu.make_async_copy(prod.at[own, :], out.at[:, chunk], s_loc.at[9])
    stay.start()
    for t in range(V):

        @pl.when(v != t)
        def _(t=t):
            home(t).start()

    gpart[v] = gsend[v]
    for s in range(V):

        @pl.when(v != s)
        def _(s=s):
            arrived(gpart.at[s], r_g.at[s]).wait()

    group = gpart[0]
    for s in range(1, V):
        group = group + gpart[s]
    gall[d] = group
    group_copies = [
        remote(gall.at[d], gall.at[d], s_q.at[k], r_q.at[d], (lax.rem(d + k, D), v)) for k in range(1, D)
    ]
    for copy in group_copies:
        copy.start()
    stay.wait()

    for t in range(V):

        @pl.when(v != t)
        def _(t=t):
            for copy in vec_copies(t):
                copy.wait_send()
            home(t).wait_send()
            inner_copy(t).wait_send()
            arrived(out.at[:, pl.ds(t * C, C)], r_o.at[t]).wait()

    @pl.when(d < D - 1)
    def _():
        cross_right.wait_send()

        @pl.when(v == V - 1)
        def _():
            crd_right.wait_send()

    @pl.when(d > 0)
    def _():
        cross_left.wait_send()

        @pl.when(v == 0)
        def _():
            crd_left.wait_send()

    for s in range(D):

        @pl.when(d != s)
        def _(s=s):
            arrived(gall.at[s], r_q.at[s]).wait()

    for copy in group_copies:
        copy.wait_send()
    whole = gall[0]
    for s in range(1, D):
        whole = whole + gall[s]
    gram[...] = whole * (1.0 / (D * PD))


def on_device(D, V, vectors, coords, leaf_basis, node_ops, top_ops, near_target, near_source, near_count):
    cols, points = vectors.shape
    rank = leaf_basis.shape[0]
    LD = points // PTS
    L = LD // V
    NC = cols * V
    C, H = L * PTS, REACH * PTS
    slots = near_target.shape[0]
    rounds = slots // LD
    toplev = top_ops.shape[0]
    base_leaf = lax.axis_index("leaf") * LD
    live = (jnp.arange(slots, dtype=jnp.int32) < near_count[0]).reshape(rounds, LD, 1)
    local = (near_target - base_leaf).reshape(rounds, LD, 1)
    shift = (near_source - near_target).reshape(rounds, LD, 1)
    hit = (local == jnp.arange(LD, dtype=jnp.int32)) & live
    offs = jnp.sum(jnp.where(hit, shift, 0), axis=1) + jnp.arange(LD, dtype=jnp.int32) % L + REACH
    offs = jnp.clip(offs, 0, L + 2 * REACH - 1).reshape(-1)
    wts = jnp.sum(jnp.where(hit, SIGNAL, 0.0).astype(F32), axis=1).reshape(-1)
    coords8 = jnp.pad(coords, ((0, 5), (0, 0)))

    def total(n):
        size = 0
        while n >= 2:
            size += n + 4
            n //= 2
        return size

    def depth(n):
        return max(1, n.bit_length() - 1)

    root_nodes = sum((D >> k) + 6 for k in range(toplev))
    dma = pltpu.SemaphoreType.DMA
    vmem = pltpu.VMEM
    scratch = [
        vmem((NC, C + 2 * H), F32),
        vmem((L + 2 * REACH, 2 * NC, PTS), BF16),
        vmem((8, C + 2 * H), F32),
        vmem((L + 2 * REACH, 3, PTS, LANES), F32),
        vmem((rank, C), F32),
        vmem(node_ops.shape, F32),
        vmem(top_ops.shape, F32),
        vmem((rounds, PTS, PTS), BF16),
        vmem((rounds, PTS, PTS), BF16),
        vmem((NC, C), F32),
        vmem((total(L), NC, LANES), F32),
        vmem((total(V), NC, LANES), F32),
        vmem((root_nodes, NC, LANES), F32),
        vmem((8, LANES), F32),
        vmem((V, cols, LANES), F32),
        vmem((V, cols, LANES), F32),
        vmem((D, cols, LANES), F32),
        dma((10,)),
        dma((3, V)),
        dma((3, V)),
        dma((2,)),
        dma((2, V)),
        dma((2,)),
        dma((2,)),
        dma((2, depth(L))),
        dma((2, depth(L))),
        dma((V,)),
        dma((V,)),
        dma((2, depth(V))),
        dma((2, depth(V))),
        dma((D,)),
        dma((D,)),
        dma((V,)),
        dma((V,)),
        dma((V,)),
        dma((V,)),
        dma((D,)),
        dma((D,)),
    ]
    smem = pl.BlockSpec(memory_space=pltpu.SMEM)
    anyw = pl.BlockSpec(memory_space=pl.ANY)
    product, gram = pl.pallas_call(
        functools.partial(kernel, (D, V, LD, rank, rounds, toplev)),
        out_shape=(
            jax.ShapeDtypeStruct((cols, points), F32),
            jax.ShapeDtypeStruct((cols, LANES), F32),
        ),
        in_specs=[smem, smem, anyw, anyw, anyw, anyw, anyw],
        out_specs=(anyw, pl.BlockSpec(memory_space=pltpu.VMEM)),
        scratch_shapes=scratch,
        compiler_params=pltpu.CompilerParams(
            collective_id=0, has_side_effects=True, vmem_limit_bytes=40 << 20
        ),
        name="hmatrix",
    )(offs, wts, vectors, coords8, leaf_basis, node_ops, top_ops)
    return product, gram[:, :NC].T


def solution(mesh):
    return jax.shard_map(
        functools.partial(on_device, mesh.shape["leaf"], mesh.shape["vec"]),
        mesh=mesh,
        in_specs=(
            P("vec", "leaf"),
            P(None, "leaf"),
            P(None, "leaf"),
            P("leaf", None, None),
            P(),
            P("leaf"),
            P("leaf"),
            P("leaf"),
        ),
        out_specs=(P("vec", "leaf"), P(None, "vec")),
        check_vma=False,
    )
```

time: 217 us -> 50.1 us (0.23)
  blocking collectives: 52.8 us -> 0 us
  matrix products: 48 us -> 0 us
  local copies, waits for them, and re-layouts: 52.2 us -> 5.01 us
  Pallas kernels: 0 us -> 42.4 us
  starting transfers between devices: 33.5 us -> 0 us
  between operations: 15.5 us -> 1.4 us
  other arithmetic: 9.62 us -> 0.98 us
  waiting for transfers between devices: 3.15 us -> 0 us
    dot_general x46 -> x0, matrix products: 48 us -> none  [the longest x8 19.2 us: add_block(): jnp.einsum('vbs,bts->bvt', source_rows[:columns], kernel, precision=EXACT...]
    pallas_call x0 -> x1, Pallas kernels: none -> 42.4 us  [on_device(): pl.pallas_call(functools.partial(kernel, (D, V, LD, rank, rounds, toplev)...]
    gather x34 -> x0, local copies, waits for them, and re-layouts: 38.5 us -> none  [the longest x8 15.9 us: add_block(): source_rows = jnp.take(window, source_ids, axis=1)]
    ppermute x12 -> x0, starting transfers between devices: 33.4 us -> none  [the longest x6 25.7 us: padded_2(): lax.ppermute(lax.slice_in_dim(block, block.shape[dim] - width, None, axis...]
    all_gather x1 -> x0, blocking collectives: 31.5 us -> none  [on_device(): all_roots = lax.all_gather(current, 'leaf', axis=0, tiled=True)]
    psum x1 -> x0, blocking collectives: 21.4 us -> none  [on_device(): gram_matrix = lax.psum(gram_part, 'leaf') / (leaf_count * points_dev)]
    reshape x9 -> x1, local copies, waits for them, and re-layouts: 5.47 us -> 0.08 us  [on_device(): wts = jnp.sum(jnp.where(hit, SIGNAL, 0.0).astype(F32), axis=1).reshape(-1)]
    gather x27 -> x0, other arithmetic: 4.91 us -> none  [the longest x10 4.81 us: take_rows(): gathered.append(padded[np.arange(count_nodes) + shift_by + pad_width])]
  transfers between devices with their start and end apart: 14 -> 0, of which waited for: 1 -> 0; matrix products, arithmetic and copies ran while one was open for 48% -> 0% of each run, Pallas kernels for 0% -> 0%
where the time goes in v1:
time: 50.1 us; the launch traced here: 49.8 us
  Pallas kernels  42.4 us (85%)
  local copies, waits for them, and re-layouts  5.01 us (10%)
  between operations  1.4 us (3%)
  other arithmetic  0.98 us (2%)
    pallas_call x1, Pallas kernels, on_device(): pl.pallas_call(functools.partial(kernel, (D, V, LD, rank, rounds, toplev)...  42.4 us
    unnamed x9, local copies, waits for them, and re-layouts  3.14 us

profile of v1, /device:TPU:0, one launch (start us, length us, event | category | flops | bytes accessed | tf_op | source)
XLA Modules:
  0.0 49.8 jit_solution(15932565239342987376)
XLA Ops:
  0.6 0.0 copy-start.2
  1.4 0.7 %broadcast_subtract_fusion = (s32[160]{0:T(256)S(1)}, s32[160]{0:T(256)S(1)}) fusion(s32[160]{0:T(256)} %param.13, s32[]{:T(128)S(6)} %mul.3, s32[160]{0:T(256)} %param.14), kind=kLoop, calls=%fused_computation.8 | loop fusion | flops 320 | bytes 2564 | tf_op jit(solution)/shard_map/sub | solution.py:614
  2.1 0.1 eq.17
  2.1 0.1 select_reduce_fusion
  2.3 0.1 reshape.38.wts
  2.3 0.1 broadcast_in_dim.24
  2.4 0.1 select_reduce_fusion.1
  2.6 0.1 min.12.offs
  2.7 0.0 copy-start.3
  2.7 1.0 %pad.4.coords = f32[8,8192]{1,0:T(8,128)S(1)} pad(f32[3,8192]{1,0:T(4,128)} %param.9, f32[]{:T(128)} %constant.34.clone.1), padding=0_5x0_0 | pad | bytes 360452 | tf_op jit(solution)/shard_map/jit(_pad)/pad | solution.py:620
  3.6 0.0 copy-done.2
  3.6 0.0 copy-done.3
  3.6 0.0 copy-start
  3.7 1.2 %copy-done = f32[32,8192]{1,0:T(8,128)S(1)} copy-done((f32[32,8192]{1,0:T(8,128)S(1)}, f32[32,8192]{1,0:T(8,128)}, u32[]{:S(2)}) %copy-start) | copy-done | bytes 1048600
  4.9 0.0 copy-start.1
  4.9 1.2 %copy-done.1 = f32[62,32,128]{2,1,0:T(8,128)S(1)} copy-done((f32[62,32,128]{2,1,0:T(8,128)S(1)}, f32[62,32,128]{2,1,0:T(8,128)}, u32[]{:S(2)}) %copy-start.1) | copy-done | bytes 1015832
  6.1 42.4 %hmatrix.1 = (f32[8,8192]{1,0:T(8,128)S(1)}, f32[8,128]{1,0:T(8,128)S(1)}) custom-call(s32[160]{0:T(256)S(1)} %min.12.offs, f32[160]{0:T(256)S(1)} %reshape.38.wts, f32[8,8192]{1,0:T(8,128)S(1)} %copy-done.2, f32[8,8192]{1,0:T(8,128)S(1)} %pad.4.coords, f32[32,8192]{1,0:T(8,128)S(1)} %copy-done, f32[62,32,128]{2,1,0:T(8,128)S(1)} %copy-done.1, ...), custom_call_target="tpu_custom_call" | custom-call | tf_op jit(solution)/shard_map/hmatrix/pallas_call | solution.py:677
  48.5 0.6 %slice_bitcast_fusion = f32[32,8]{0,1:T(8,128)} fusion(f32[8,128]{1,0:T(8,128)S(1)} %get-tuple-element.5), kind=kLoop, calls=%fused_computation.4 | loop fusion | bytes 2048 | tf_op jit(solution)/shard_map/transpose | solution.py:691
  49.1 0.7 %copy.12 = f32[8,8192]{1,0:T(8,128)} copy(f32[8,8192]{1,0:T(8,128)S(1)} %get-tuple-element.10) | data formatting | bytes 524288
  (3 shorter events, 0.0 us)
Async XLA Ops:
  0.6 3.0 %copy-start.2 = (f32[8,8192]{1,0:T(8,128)S(1)}, f32[8,8192]{1,0:T(8,128)}, u32[]{:S(2)}) copy-start(f32[8,8192]{1,0:T(8,128)} %vecs.1) | copy-start | bytes 786436
  2.7 1.0 %copy-start.3 = (f32[2,32,192]{2,1,0:T(8,128)S(1)}, f32[2,32,192]{2,1,0:T(8,128)}, u32[]{:S(2)}) copy-start(f32[2,32,192]{2,1,0:T(8,128)} %tops.1) | copy-start | bytes 147460
  3.6 1.2 %copy-start = (f32[32,8192]{1,0:T(8,128)S(1)}, f32[32,8192]{1,0:T(8,128)}, u32[]{:S(2)}) copy-start(f32[32,8192]{1,0:T(8,128)} %basis.1) | copy-start | bytes 3145732
  4.9 1.2 %copy-start.1 = (f32[62,32,128]{2,1,0:T(8,128)S(1)}, f32[62,32,128]{2,1,0:T(8,128)}, u32[]{:S(2)}) copy-start(f32[62,32,128]{2,1,0:T(8,128)} %ops.1) | copy-start | bytes 3047428

commit v2 on v1

--- a/solution.py
+++ b/solution.py
@@ -230,6 +230,33 @@
         for copy in high_loads:
             copy.wait()
 
+    origin = (g * L).astype(F32) * SLAB
+
+    def scale_points(lo, size):
+        points = crd[:, lo : lo + size]
+        first = lax.broadcasted_iota(jnp.int32, points.shape, 0) == 0
+        crd[:, lo : lo + size] = (points - jnp.where(first, origin, 0.0)) * SCALE
+
+    def spread_leaves(lo, count):
+        pack = 4
+
+        def spread(i, carry):
+            for j in range(pack):
+                leaf = lo + i * pack + j
+                for half in range(PTS // LANES):
+                    at = pl.ds(pl.multiple_of(leaf * PTS + half * LANES, LANES), LANES)
+                    tall = crd[:, at].T
+                    for axis in range(3):
+                        bcol[leaf, axis, half * LANES : (half + 1) * LANES, :] = jnp.broadcast_to(
+                            tall[:, axis : axis + 1], (LANES, LANES)
+                        )
+            return carry
+
+        lax.fori_loop(0, count // pack, spread, 0)
+
+    scale_points(H, C)
+    spread_leaves(REACH, L)
+
     for s in range(V):
         rows = pl.ds(s * cols, cols)
 
@@ -316,20 +343,10 @@
     def _():
         arrived(crd.at[:, pl.ds(H + C, H)], r_c.at[1]).wait()
 
-    origin = (g * L).astype(F32) * SLAB
-    first = lax.broadcasted_iota(jnp.int32, crd.shape, 0) == 0
-    crd[...] = (crd[...] - jnp.where(first, origin, 0.0)) * SCALE
-
-    def spread(i, carry):
-        at = pl.ds(pl.multiple_of(i * LANES, LANES), LANES)
-        tall = crd[:, at].T
-        for axis in range(3):
-            bcol[i // 2, axis, pl.ds(pl.multiple_of(lax.rem(i, 2) * LANES, LANES), LANES), :] = jnp.broadcast_to(
-                tall[:, axis : axis + 1], (LANES, LANES)
-            )
-        return carry
-
-    lax.fori_loop(0, (C + 2 * H) // LANES, spread, 0)
+    scale_points(0, H)
+    scale_points(H + C, H)
+    spread_leaves(0, REACH)
+    spread_leaves(REACH + L, REACH)
 
     for leaf in range(L + 2 * REACH):
         high, low = halves(win[:, leaf * PTS : (leaf + 1) * PTS])
@@ -684,7 +701,7 @@
         out_specs=(anyw, pl.BlockSpec(memory_space=pltpu.VMEM)),
         scratch_shapes=scratch,
         compiler_params=pltpu.CompilerParams(
-            collective_id=0, has_side_effects=True, vmem_limit_bytes=40 << 20
+            collective_id=0, has_side_effects=True, vmem_limit_bytes=67043328
         ),
         name="hmatrix",
     )(offs, wts, vectors, coords8, leaf_basis, node_ops, top_ops)

time: 50.1 us -> 45 us (0.90)
  Pallas kernels: 42.4 us -> 36.4 us
  local copies, waits for them, and re-layouts: 5.01 us -> 6.68 us
  other arithmetic: 0.98 us -> 0.28 us
    pallas_call x1, Pallas kernels: 42.4 us -> 36.4 us  [on_device(): pl.pallas_call(functools.partial(kernel, (D, V, LD, rank, rounds, toplev)...]
    unnamed x9 -> x5, local copies, waits for them, and re-layouts: 3.14 us -> 2.33 us
    sub x1, other arithmetic: 0.7 us -> 0.01 us  [on_device(): local = (near_target - base_leaf).reshape(rounds, LD, 1)]
    transpose x1, local copies, waits for them, and re-layouts: 0.6 us -> 1.27 us  [on_device(): return (product, gram[:, :NC].T)]
    pad x1, local copies, waits for them, and re-layouts: 0.96 us -> 1.63 us  [on_device(): coords8 = jnp.pad(coords, ((0, 5), (0, 0)))]
    reshape x1, local copies, waits for them, and re-layouts: 0.08 us -> 0.66 us  [on_device(): wts = jnp.sum(jnp.where(hit, SIGNAL, 0.0).astype(F32), axis=1).reshape(-1)]
    min x1, local copies, waits for them, and re-layouts: 0.08 us -> 0.64 us  [on_device(): offs = jnp.clip(offs, 0, L + 2 * REACH - 1).reshape(-1)]
where the time goes in v2:
time: 45 us; the launch traced here: 44.7 us
  Pallas kernels  36.4 us (81%)
  local copies, waits for them, and re-layouts  6.68 us (15%)
  between operations  1.34 us (3%)
    pallas_call x1, Pallas kernels, on_device(): pl.pallas_call(functools.partial(kernel, (D, V, LD, rank, rounds, toplev)...  36.4 us
    unnamed x5, local copies, waits for them, and re-layouts  2.33 us
    pad x1, local copies, waits for them, and re-layouts, on_device(): coords8 = jnp.pad(coords, ((0, 5), (0, 0)))  1.63 us
    transpose x1, local copies, waits for them, and re-layouts, on_device(): return (product, gram[:, :NC].T)  1.27 us

profile of v2, /device:TPU:0, one launch (start us, length us, event | category | flops | bytes accessed | tf_op | source)
XLA Modules:
  0.0 44.7 jit_solution(10707957324777872846)
XLA Ops:
  1.3 0.0 copy-start.1
  1.3 0.0 copy-start
  1.3 0.6 %copy-done.1 = s32[160]{0:T(256)S(1)} copy-done((s32[160]{0:T(256)S(1)}, s32[160]{0:T(256)}, u32[]{:S(2)}) %copy-start.1) | copy-done | bytes 664
  2.0 0.0 copy-done
  2.0 0.1 eq.17
  2.1 0.1 select_reduce_fusion
  2.2 0.7 %reshape.38.wts = f32[160]{0:T(256)} reshape(f32[5,32]{1,0:T(8,128)S(1)} %select_reduce_fusion) | data formatting | bytes 1280 | tf_op jit(solution)/shard_map/reshape | solution.py:636
  2.9 0.1 broadcast_in_dim.24
  2.9 0.1 select_reduce_fusion.1
  3.1 0.6 %min.12.offs = s32[160]{0:T(256)} reshape(s32[5,32]{1,0:T(8,128)S(1)} %add_clamp_fusion) | data formatting | bytes 1280 | tf_op jit(solution)/shard_map/jit(clip)/min | solution.py:635
  3.7 1.6 %pad.4.coords = f32[8,8192]{1,0:T(8,128)} pad(f32[3,8192]{1,0:T(4,128)} %param.9, f32[]{:T(128)} %constant.34.clone.1), padding=0_5x0_0 | pad | bytes 360452 | tf_op jit(solution)/shard_map/jit(_pad)/pad | solution.py:637
  5.4 36.4 %hmatrix.1 = (f32[8,8192]{1,0:T(8,128)}, f32[8,128]{1,0:T(8,128)}) custom-call(s32[160]{0:T(256)} %min.12.offs, f32[160]{0:T(256)} %reshape.38.wts, f32[8,8192]{1,0:T(8,128)} %vecs.1, f32[8,8192]{1,0:T(8,128)} %pad.4.coords, f32[32,8192]{1,0:T(8,128)} %basis.1, f32[62,32,128]{2,1,0:T(8,128)} %ops.1, f32[2,32,192]{2,1,0:T(8,128)} %tops.1), custom_call_target="tpu_custom_call" | custom-call | tf_op jit(solution)/shard_map/hmatrix/pallas_call | solution.py:694
  41.8 1.3 %slice_bitcast_fusion = f32[32,8]{0,1:T(8,128)} fusion(f32[8,128]{1,0:T(8,128)} %get-tuple-element.5), kind=kLoop, calls=%fused_computation.4 | loop fusion | bytes 2048 | tf_op jit(solution)/shard_map/transpose | solution.py:708
  43.1 1.7 %copy.12 = f32[8,8192]{1,0:T(8,128)} copy(f32[8,8192]{1,0:T(8,128)} %get-tuple-element.10) | data formatting | bytes 524288
  (4 shorter events, 0.0 us)
Async XLA Ops:
  1.3 0.7 %copy-start.1 = (s32[160]{0:T(256)S(1)}, s32[160]{0:T(256)}, u32[]{:S(2)}) copy-start(s32[160]{0:T(256)} %param.14) | copy-start | bytes 1924
  1.3 0.7 %copy-start = (s32[160]{0:T(256)S(1)}, s32[160]{0:T(256)}, u32[]{:S(2)}) copy-start(s32[160]{0:T(256)} %param.13) | copy-start | bytes 1924

commit v3 on v2

--- a/solution.py
+++ b/solution.py
@@ -634,7 +634,6 @@
     offs = jnp.sum(jnp.where(hit, shift, 0), axis=1) + jnp.arange(LD, dtype=jnp.int32) % L + REACH
     offs = jnp.clip(offs, 0, L + 2 * REACH - 1).reshape(-1)
     wts = jnp.sum(jnp.where(hit, SIGNAL, 0.0).astype(F32), axis=1).reshape(-1)
-    coords8 = jnp.pad(coords, ((0, 5), (0, 0)))
 
     def total(n):
         size = 0
@@ -652,7 +651,7 @@
     scratch = [
         vmem((NC, C + 2 * H), F32),
         vmem((L + 2 * REACH, 2 * NC, PTS), BF16),
-        vmem((8, C + 2 * H), F32),
+        vmem((3, C + 2 * H), F32),
         vmem((L + 2 * REACH, 3, PTS, LANES), F32),
         vmem((rank, C), F32),
         vmem(node_ops.shape, F32),
@@ -704,7 +703,7 @@
             collective_id=0, has_side_effects=True, vmem_limit_bytes=67043328
         ),
         name="hmatrix",
-    )(offs, wts, vectors, coords8, leaf_basis, node_ops, top_ops)
+    )(offs, wts, vectors, coords, leaf_basis, node_ops, top_ops)
     return product, gram[:, :NC].T
 
 

time: 45 us -> 43.1 us (0.958)
  local copies, waits for them, and re-layouts: 6.68 us -> 5.04 us
    pad x1 -> x0, local copies, waits for them, and re-layouts: 1.63 us -> none  [on_device(): coords8 = jnp.pad(coords, ((0, 5), (0, 0)))]
where the time goes in v3:
time: 43.1 us; the launch traced here: 42.9 us
  Pallas kernels  36.2 us (84%)
  local copies, waits for them, and re-layouts  5.04 us (12%)
  between operations  1.34 us (3%)
    pallas_call x1, Pallas kernels, on_device(): pl.pallas_call(functools.partial(kernel, (D, V, LD, rank, rounds, toplev)...  36.2 us
    unnamed x5, local copies, waits for them, and re-layouts  2.33 us
    transpose x1, local copies, waits for them, and re-layouts, on_device(): return (product, gram[:, :NC].T)  1.27 us

profile of v3, /device:TPU:0, one launch (start us, length us, event | category | flops | bytes accessed | tf_op | source)
XLA Modules:
  0.0 42.9 jit_solution(3212965054989111197)
XLA Ops:
  1.3 0.0 copy-start.1
  1.3 0.0 copy-start
  1.3 0.6 %copy-done.1 = s32[160]{0:T(256)S(1)} copy-done((s32[160]{0:T(256)S(1)}, s32[160]{0:T(256)}, u32[]{:S(2)}) %copy-start.1) | copy-done | bytes 664
  2.0 0.0 copy-done
  2.0 0.1 eq.17
  2.1 0.1 select_reduce_fusion
  2.2 0.6 %reshape.38.wts = f32[160]{0:T(256)} reshape(f32[5,32]{1,0:T(8,128)S(1)} %select_reduce_fusion) | data formatting | bytes 1280 | tf_op jit(solution)/shard_map/reshape | solution.py:636
  2.8 0.1 broadcast_in_dim.24
  2.9 0.1 select_reduce_fusion.1
  3.1 0.6 %min.12.offs = s32[160]{0:T(256)} reshape(s32[5,32]{1,0:T(8,128)S(1)} %add_clamp_fusion) | data formatting | bytes 1280 | tf_op jit(solution)/shard_map/jit(clip)/min | solution.py:635
  3.7 36.2 %hmatrix.1 = (f32[8,8192]{1,0:T(8,128)}, f32[8,128]{1,0:T(8,128)}) custom-call(s32[160]{0:T(256)} %min.12.offs, f32[160]{0:T(256)} %reshape.38.wts, f32[8,8192]{1,0:T(8,128)} %vecs.1, f32[3,8192]{1,0:T(4,128)} %coords.1, f32[32,8192]{1,0:T(8,128)} %basis.1, f32[62,32,128]{2,1,0:T(8,128)} %ops.1, f32[2,32,192]{2,1,0:T(8,128)} %tops.1), custom_call_target="tpu_custom_call" | custom-call | tf_op jit(solution)/shard_map/hmatrix/pallas_call | solution.py:693
  40.0 1.3 %slice_bitcast_fusion = f32[32,8]{0,1:T(8,128)} fusion(f32[8,128]{1,0:T(8,128)} %get-tuple-element.5), kind=kLoop, calls=%fused_computation.4 | loop fusion | bytes 2048 | tf_op jit(solution)/shard_map/transpose | solution.py:707
  41.2 1.7 %copy.12 = f32[8,8192]{1,0:T(8,128)} copy(f32[8,8192]{1,0:T(8,128)} %get-tuple-element.10) | data formatting | bytes 524288
  (4 shorter events, 0.0 us)
Async XLA Ops:
  1.3 0.7 %copy-start.1 = (s32[160]{0:T(256)S(1)}, s32[160]{0:T(256)}, u32[]{:S(2)}) copy-start(s32[160]{0:T(256)} %param.14) | copy-start | bytes 1924
  1.3 0.7 %copy-start = (s32[160]{0:T(256)S(1)}, s32[160]{0:T(256)}, u32[]{:S(2)}) copy-start(s32[160]{0:T(256)} %param.13) | copy-start | bytes 1924
